TPU v7x, 32 devices: a whole 2x2x4 slice. The times are simulated.
32 devices in a mesh: sec: 2 (over y), dev: 16 (over z, x, core).
Axes of the slice: x: 2, y: 2, z: 4, core: 2. Of those that a mesh axis runs over, the one named last changes fastest.
Arguments:
- flow_state: float32 [5, 8, 1024, 512], P(None, None, ('sec', 'dev')), may hold values from -6 to 6
- diffusion: float32 [8, 1024, 512], P(None, ('sec', 'dev')), may hold values from 0.02 to 0.1
- wall_stress: float32 [2, 1024, 512], P(None, ('sec', 'dev')), may hold values from -3 to 3
- batch_counts: int32 [32, 48], P(('sec', 'dev')), may hold values from 1 to 4, 120 in all within a row
- batch_routes: int32 [1536, 1], P(('sec', 'dev')), may hold values from 0 to 31; in each aligned block of 48 rows (0 to 47, 48 to 95, ...) at most 2 rows name the same one
- wall_index: int32 [1536, 4], P(('sec', 'dev')), may hold values from 0 to 16383, as said below
- input_weight: bfloat16 [12, 2048], replicated, may hold values from -1.75 to 1.75
- middle_weight: bfloat16 [2048, 2048], P(('sec', 'dev')), may hold values from -0.125 to 0.125
- output_weight: bfloat16 [2, 2048], replicated, may hold values from -0.125 to 0.125
Outputs:
- new_field: float32 [5, 8, 1024, 512], P(None, None, ('sec', 'dev'))
- new_stress: float32 [2, 1024, 512], P(None, ('sec', 'dev'))
- batch_loss: float32 [32], P(('sec', 'dev'))
- grad_w_in: float32 [12, 2048], replicated
- grad_w_mid: float32 [2048, 2048], P(('sec', 'dev'))
Inputs may be any that keep to these rules, and one draw needn't show every extreme that they name: `batch_routes`: within the 48 rows of one device no trainer is named more than 2 times, and every trainer is named by some row. `batch_counts`: each device's row sums to 120. `wall_index`: all entries of the 48 rows of one device are distinct.
All inputs are finite; a program needn't handle non-finite values.
Results may differ from a plain program's by a relative error of at most 0.00091.
Values may be sent and summed in bfloat16 or wider, within the bound.
No kernel may reach another device: no remote copies, remote signals or barrier semaphores. Data moves between devices by JAX's collectives and lax.ppermute only.
A program may use at most 128 MiB of HBM per device.

v0:
```python
import math
import jax
import jax.numpy as jnp
from jax import lax
from jax.sharding import PartitionSpec as P

SLOTS = 2
advect_number = 0.3
wall_gain = 0.5
grad_number = 32.0


def extended(block, sides, width):
    for axis, dim in sides:
        count = lax.axis_size(axis)
        forward = [(i, i + 1) for i in range(count - 1)]
        forward.append((count - 1, 0))
        backward = [(target, source) for source, target in forward]
        low = lax.ppermute(
            lax.slice_in_dim(block, block.shape[dim] - width, None, axis=dim), axis, forward
        )
        high = lax.ppermute(lax.slice_in_dim(block, 0, width, axis=dim), axis, backward)
        block = jnp.concatenate([low, block, high], axis=dim)
    return block


def advance(flow_state, diffusion, below_z, above_z):
    below_x = jnp.concatenate([flow_state[..., :1], flow_state[..., :-1]], axis=3)
    above_x = jnp.concatenate([flow_state[..., 1:], flow_state[..., -1:]], axis=3)
    below_y = jnp.concatenate([flow_state[:, :1], flow_state[:, :-1]], axis=1)
    above_y = jnp.concatenate([flow_state[:, 1:], flow_state[:, -1:]], axis=1)
    spread = below_x + above_x + below_y + above_y + below_z + above_z - 6.0 * flow_state
    return flow_state + advect_number * (below_x - flow_state) + diffusion[None] * spread


def wall_columns(flow_state):
    points = flow_state.shape[2] * flow_state.shape[3]
    inputs = flow_state[0:4, 0:3].reshape(12, points)
    targets = jnp.stack(
        [flow_state[1, 4] - flow_state[1, 3], flow_state[3, 4] - flow_state[3, 3]]
    ).reshape(2, points)
    return jnp.concatenate([inputs, targets], axis=0).astype(jnp.bfloat16)


def apply_wall(advanced, new_stress):
    advanced = advanced.at[1, 0].add(-wall_gain * new_stress[0])
    return advanced.at[3, 0].add(-wall_gain * new_stress[1])


def contract_first(left, right):
    return lax.dot_general(
        left, right, (((0,), (0,)), ((), ())), preferred_element_type=jnp.float32
    )


def contract_last(left, right):
    return lax.dot_general(
        left, right, (((1,), (1,)), ((), ())), preferred_element_type=jnp.float32
    )


def body(
    flow_state,
    diffusion,
    wall_stress,
    batch_counts,
    batch_routes,
    wall_index,
    input_weight,
    middle_weight,
    output_weight,
):
    tile_count, capacity = wall_index.shape
    devices = lax.axis_size(("sec", "dev"))
    channels = 14
    slot_total = devices * SLOTS
    row_total = slot_total * capacity
    points = flow_state.shape[2] * flow_state.shape[3]
    columns = wall_columns(flow_state)
    picked = jnp.take(columns, wall_index.reshape(-1), axis=1).reshape(
        channels, tile_count, capacity
    )
    is_live = (
        jnp.arange(capacity, dtype=jnp.int32)[None, :] < batch_counts.reshape(tile_count)[:, None]
    )
    picked = jnp.where(is_live[None], picked, jnp.zeros((), jnp.bfloat16))
    destination = batch_routes.reshape(tile_count)
    matches = (destination[:, None] == jnp.arange(devices, dtype=jnp.int32)[None, :]).astype(
        jnp.int32
    )
    slot_rank = jnp.sum((jnp.cumsum(matches, axis=0) - matches) * matches, axis=1)
    slot_id = destination * SLOTS + slot_rank
    placing = (slot_id[:, None] == jnp.arange(slot_total, dtype=jnp.int32)[None, :]).astype(
        jnp.bfloat16
    )
    send_rows = jnp.einsum(
        "bs,cbk->sck", placing, picked, preferred_element_type=jnp.float32
    ).astype(jnp.bfloat16)
    send_rows = send_rows.reshape(devices, SLOTS, channels, capacity)
    send_live = jnp.einsum(
        "bs,bk->sk", placing, is_live.astype(jnp.bfloat16), preferred_element_type=jnp.float32
    ).astype(jnp.bfloat16)
    send_live = send_live.reshape(devices, SLOTS, capacity)
    got_rows, got_live = (
        lax.all_to_all(send_rows, ("sec", "dev"), split_axis=0, concat_axis=0, tiled=True),
        lax.all_to_all(send_live, ("sec", "dev"), split_axis=0, concat_axis=0, tiled=True),
    )
    sample_rows = jnp.transpose(got_rows, (0, 1, 3, 2)).reshape(row_total, channels)
    features = sample_rows[:, :12]
    targets = sample_rows[:, 12:].astype(jnp.float32)
    live_rows = got_live.reshape(row_total).astype(jnp.float32)
    pre_first = jnp.dot(features, input_weight, preferred_element_type=jnp.float32)
    first_tanh = jnp.tanh(pre_first)
    first_act = first_tanh.astype(jnp.bfloat16)
    part = first_act
    pre_second = jnp.dot(
        part,
        lax.all_gather(middle_weight, ("sec", "dev"), axis=0, tiled=True),
        preferred_element_type=jnp.float32,
    )
    second_tanh = jnp.tanh(pre_second)
    second_act = second_tanh.astype(jnp.bfloat16)
    prediction = contract_last(second_act, output_weight)
    errors = (prediction - targets) * live_rows[:, None]
    sent_back = jnp.transpose(
        prediction.astype(jnp.bfloat16).reshape(devices, SLOTS, capacity, 2), (0, 1, 3, 2)
    )
    answers = lax.all_to_all(sent_back, ("sec", "dev"), split_axis=0, concat_axis=0, tiled=True)
    answers = answers.reshape(slot_total, 2, capacity)
    live_total = jnp.sum(live_rows)
    batch_loss = (0.5 * jnp.sum(errors * errors) / live_total).reshape(1)
    live_dev = 5 * tile_count * capacity // 8
    scale = grad_number / math.sqrt(live_dev * devices)
    back_out = (errors * scale).astype(jnp.bfloat16)
    back_second = (
        jnp.dot(back_out, output_weight, preferred_element_type=jnp.float32)
        * (1.0 - second_tanh * second_tanh)
    ).astype(jnp.bfloat16)
    back_hidden = contract_last(
        back_second, lax.all_gather(middle_weight, ("sec", "dev"), axis=0, tiled=True)
    )
    back_first = (back_hidden * (1.0 - first_tanh * first_tanh)).astype(jnp.bfloat16)
    part = first_act
    grad_w_mid = lax.psum_scatter(
        contract_first(part, back_second), ("sec", "dev"), scatter_dimension=0, tiled=True
    )
    grad_w_in = lax.psum(contract_first(features, back_first), ("sec", "dev"))
    per_tile = jnp.einsum("bs,sck->cbk", placing, answers, preferred_element_type=jnp.float32)
    target_index = jnp.where(is_live, wall_index, points).reshape(-1)
    new_stress = (
        wall_stress.reshape(2, points)
        .at[:, target_index]
        .set(per_tile.reshape(2, -1), mode="drop")
        .reshape(wall_stress.shape)
    )
    padded = extended(flow_state.astype(jnp.bfloat16), ((("sec", "dev"), 2),), 1).astype(
        flow_state.dtype
    )
    advanced = advance(flow_state, diffusion, padded[:, :, :-2], padded[:, :, 2:])
    new_field = apply_wall(advanced, new_stress)
    return (new_field, new_stress, batch_loss, grad_w_in, grad_w_mid)


def solution(mesh):
    in_specs = (
        P(None, None, ("sec", "dev"), None),
        P(None, ("sec", "dev"), None),
        P(None, ("sec", "dev"), None),
        P(("sec", "dev"), None),
        P(("sec", "dev"), None),
        P(("sec", "dev"), None),
        P(),
        P(("sec", "dev"), None),
        P(),
    )
    out_specs = (
        P(None, None, ("sec", "dev"), None),
        P(None, ("sec", "dev"), None),
        P(("sec", "dev")),
        P(),
        P(("sec", "dev"), None),
    )
    return jax.shard_map(body, mesh=mesh, in_specs=in_specs, out_specs=out_specs, check_vma=False)
```

profile of v0, /device:TPU:9, one launch (start us, length us, event | category | flops | bytes accessed | tf_op | source)
XLA Modules:
  0.0 425.7 jit_solution(3434637611886213195)
XLA Ops:
  7.2 0.7 all-gather.2.cloned.1.call-update
  7.9 0.8 fusion.25
  8.8 0.8 select_reduce_fusion
  9.6 0.7 fusion.36
  10.3 0.8 convolution_convert_fusion.1
  11.2 0.7 copy.49
  11.9 6.3 %all-to-all-start.2 = ((bf16[32,2,4]{2,1,0:T(2,128)(2,1)}), bf16[32,2,4]{2,1,0:T(2,128)(2,1)S(1)}, u32[]{:S(2)}, u32[]{:S(2)}) async-start(bf16[32,2,4]{2,1,0:T(2,128)(2,1)} %bitcast.18), calls=%async_computation.2 | async-start | bytes 32768 | tf_op jit(solution)/shard_map/all_to_all | solution.py:106
  18.2 0.8 copy.37
  19.1 2.0 convert_element_type.52
  21.3 1.0 copy-done.3
  22.3 0.3 copy.53
  22.6 0.2 pad_maximum_fusion.1
  22.9 3.4 copy.38
  26.3 3.4 gather_fusion
  29.8 0.2 convolution_convert_fusion
  30.0 0.1 copy.40
  30.2 0.7 copy.41
  30.8 5.8 %all-to-all-start = ((bf16[32,2,14,4]{2,1,3,0:T(2,128)(2,1)}), bf16[32,2,14,4]{2,1,3,0:T(2,128)(2,1)S(1)}, u32[]{:S(2)}, u32[]{:S(2)}) async-start(bf16[32,2,14,4]{2,1,3,0:T(2,128)(2,1)} %copy.41), calls=%async_computation | async-start | bytes 131072 | tf_op jit(solution)/shard_map/all_to_all | solution.py:105
  36.9 5.8 %all-to-all-done = bf16[32,2,14,4]{2,1,3,0:T(2,128)(2,1)S(1)} async-done(((bf16[32,2,14,4]{2,1,3,0:T(2,128)(2,1)}), bf16[32,2,14,4]{2,1,3,0:T(2,128)(2,1)S(1)}, u32[]{:S(2)}, u32[]{:S(2)}) %all-to-all-start) | async-done | bytes 7200 | tf_op jit(solution)/shard_map/all_to_all | solution.py:105
  42.9 1.8 convolution_tanh_fusion.1
  44.6 44.9 %all-gather.2.cloned.1.call-done = bf16[2048,2048]{1,0:T(8,128)(2,1)} async-done(((bf16[64,2048]{1,0:T(8,128)(2,1)}), bf16[2048,2048]{1,0:T(8,128)(2,1)}) %all-gather.2.cloned.1.call-update) | async-done | bytes 8388624 | tf_op jit(solution)/shard_map/all_gather | solution.py:118
  89.6 6.4 %convolution_tanh_fusion = f32[256,2048]{1,0:T(8,128)S(1)} fusion(bf16[2048,2048]{1,0:T(8,128)(2,1)} %all-gather.2.cloned.1.call-done, f32[256,2048]{1,0:T(8,128)} %convolution_tanh_fusion.1), kind=kOutput, calls=%fused_computation.8 | convolution fusion | flops 2148007936 | bytes 12582912 | tf_op jit(solution)/shard_map/dot_general | solution.py:116
  96.0 1.0 multiply_reduce_fusion
  97.0 1.5 fusion.8
  98.4 7.4 %fusion.9 = f32[12,2048]{1,0:T(8,128)} fusion(bf16[256,2048]{1,0:T(8,128)(2,1)} %fusion.8, bf16[2048,2048]{1,0:T(8,128)(2,1)} %all-gather.2.cloned.1.call-done, f32[256,2048]{1,0:T(8,128)} %convolution_tanh_fusion.1, bf16[256,14]{1,0:T(8,128)(2,1)S(1)} %bitcast.59), kind=kOutput, calls=%fused_computation.22 | convolution fusion | flops 2162163712 | bytes 11639808 | tf_op jit(solution)/shard_map/dot_general | solution.py:51
  105.9 10.0 %fusion.13 = f32[2048,2048]{1,0:T(8,128)} fusion(bf16[256,2048]{1,0:T(8,128)(2,1)} %fusion.8, f32[256,2048]{1,0:T(8,128)} %convolution_tanh_fusion.1), kind=kOutput, calls=%fused_computation.30 | convolution fusion | flops 2148007936 | bytes 19922944 | tf_op jit(solution)/shard_map/dot_general | solution.py:51
  115.9 1.3 fusion.45
  117.2 1.3 collective-permute-start
  118.7 4.6 %copy.35 = f32[2,32,512]{0,2,1:T(8,128)} copy(f32[2,32,512]{2,1,0:T(8,128)S(1)} %copy-done.5) | data formatting | bytes 262144 | tf_op args[2]
  123.4 0.9 fusion.44
  124.3 1.1 fusion.41
  125.4 2.8 fusion.43
  128.2 3.4 fusion.42
  131.7 0.6 convert_reduce_fusion
  132.3 3.4 maximum_convert_fusion
  135.8 0.6 copy.43
  136.4 6.6 %all-to-all-start.1 = ((bf16[32,2,2,4]{3,1,2,0:T(2,128)(2,1)}), bf16[32,2,2,4]{3,1,2,0:T(2,128)(2,1)S(1)}, u32[]{:S(2)}, u32[]{:S(2)}) async-start(bf16[32,2,2,4]{3,1,2,0:T(2,128)(2,1)} %copy.43), calls=%async_computation.1 | async-start | bytes 65536 | tf_op jit(solution)/shard_map/all_to_all | solution.py:128
  143.1 9.2 %fusion.4 = f32[5,8,32,512]{3,2,1,0:T(8,128)} fusion(f32[5,8,34,512]{3,2,1,0:T(8,128)} %maximum_convert_fusion, f32[5,8,32,1]{3,2,1,0:T(8,128)} %get-tuple-element.49, f32[5,8,32,511]{3,2,1,0:T(8,128)} %get-tuple-element.51, f32[5,7,32,512]{3,2,1,0:T(8,128)} %get-tuple-element.53, f32[5,1,32,512]{3,2,1,0:T(8,128)} %get-tuple-element.55, ...), kind=kLoop, calls=%fused_computation.13 | loop fusion | flops 10485760 | bytes 21495808 | tf_op jit(solution)/shard_map/add | solution.py:33
  153.7 0.2 convolution_bitcast_fusion
  154.1 0.1 copy.47
  154.2 7.6 %scatter_fusion = f32[2,16384]{0,1:T(8,128)} fusion(f32[2,16384]{0,1:T(8,128)} %bitcast.52, s32[192]{0:T(256)S(1)} %bitcast.68, f32[192,2]{1,0:T(8,128)S(1)} %copy.47), kind=kCustom, calls=%fused_computation.1 | custom fusion | bytes 5376 | tf_op jit(solution)/shard_map/scatter | solution.py:153
  161.8 5.9 %copy.50 = f32[2,32,512]{2,1,0:T(8,128)} copy(f32[2,32,512]{0,2,1:T(8,128)} %bitcast.53) | data formatting | bytes 262144
  167.7 12.3 %fusion = (f32[16384]{0:T(1024)S(1)}, f32[16384]{0:T(1024)S(1)}) fusion(f32[2,16384]{0,1:T(8,128)} %scatter_fusion), kind=kLoop, calls=%fused_computation.3 | loop fusion | flops 32768 | bytes 262144 | tf_op jit(solution)/shard_map/mul | solution.py:47
  180.0 1.5 fusion.17
  181.5 1.5 fusion.16
  183.0 43.7 %all-reduce.2.cloned.1.call-done = f32[12,2048]{1,0:T(8,128)} async-done(((f32[12,2048]{1,0:T(8,128)}), f32[12,2048]{1,0:T(8,128)}) %all-reduce.2.cloned.1.call-update) | async-done | bytes 98320 | tf_op jit(solution)/shard_map/psum | solution.py:147
  226.7 189.8 %reduce-scatter.2.cloned.1.call-done = f32[64,2048]{1,0:T(8,128)} async-done(((f32[2048,2048]{1,0:T(8,128)}), f32[64,2048]{1,0:T(8,128)}) %reduce-scatter.2.cloned.1.call-update) | async-done | bytes 524304 | tf_op jit(solution)/shard_map/reduce_scatter | solution.py:144
  416.5 1.6 copy.60
  (52 shorter events, 1.6 us)
Async XLA Ops:
  7.2 35.7 %copy-start = (bf16[12,2048]{1,0:T(8,128)(2,1)S(1)}, bf16[12,2048]{1,0:T(8,128)(2,1)}, u32[]{:S(2)}) copy-start(bf16[12,2048]{1,0:T(8,128)(2,1)} %param.19) | copy-start | bytes 147460
  7.2 13.9 %copy-start.2 = (f32[5,8,32,512]{3,2,1,0:T(8,128)S(1)}, f32[5,8,32,512]{3,2,1,0:T(8,128)}, u32[]{:S(2)}) copy-start(f32[5,8,32,512]{3,2,1,0:T(8,128)} %param.13) | copy-start | bytes 7864324
  7.2 82.4 %all-gather.2.cloned.1.call-start = ((), (), s32[]{:S(2)}) async-start(), calls=%async_computation.4 | async-start | bytes 8650752 | tf_op jit(solution)/shard_map/all_gather | solution.py:118
  11.9 19.0 %all-to-all-start.2 = ((bf16[32,2,4]{2,1,0:T(2,128)(2,1)}), bf16[32,2,4]{2,1,0:T(2,128)(2,1)S(1)}, u32[]{:S(2)}, u32[]{:S(2)}) async-start(bf16[32,2,4]{2,1,0:T(2,128)(2,1)} %bitcast.18), calls=%async_computation.2 | async-start | bytes 32768 | tf_op jit(solution)/shard_map/all_to_all | solution.py:106
  21.1 1.2 copy-start.3
  22.9 6.9 %copy-start.7 = (s32[48,4]{0,1:T(4,128)S(1)}, s32[48,4]{0,1:T(4,128)}, u32[]{:S(2)}) copy-start(s32[48,4]{0,1:T(4,128)} %param.18) | copy-start | bytes 2308
  22.9 6.9 %copy-start.8 = (s32[1,48]{1,0:T(1,128)S(1)}, s32[1,48]{1,0:T(1,128)}, u32[]{:S(2)}) copy-start(s32[1,48]{1,0:T(1,128)} %param.16) | copy-start | bytes 580
  30.8 11.8 %all-to-all-start = ((bf16[32,2,14,4]{2,1,3,0:T(2,128)(2,1)}), bf16[32,2,14,4]{2,1,3,0:T(2,128)(2,1)S(1)}, u32[]{:S(2)}, u32[]{:S(2)}) async-start(bf16[32,2,14,4]{2,1,3,0:T(2,128)(2,1)} %copy.41), calls=%async_computation | async-start | bytes 131072 | tf_op jit(solution)/shard_map/all_to_all | solution.py:105
  36.7 190.0 %all-reduce.2.cloned.1.call-start = ((), (), s32[]{:S(2)}) async-start(), calls=%async_computation.5 | async-start | bytes 262144 | tf_op jit(solution)/shard_map/psum | solution.py:147
  44.6 51.3 %copy-start.6 = (bf16[2,2048]{1,0:T(2,128)(2,1)S(1)}, bf16[2,2048]{1,0:T(2,128)(2,1)}, u32[]{:S(2)}) copy-start(bf16[2,2048]{1,0:T(2,128)(2,1)} %param.21) | copy-start | bytes 24580
  105.9 310.7 %reduce-scatter.2.cloned.1.call-start = ((), (), s32[]{:S(2)}) async-start(), calls=%async_computation.6 | async-start | bytes 17301504 | tf_op jit(solution)/shard_map/reduce_scatter | solution.py:144
  115.9 2.8 copy-start.5
  117.2 15.1 %collective-permute-start = (bf16[5,8,1,512]{3,2,1,0:T(2,128)(2,1)S(1)}, bf16[5,8,1,512]{3,2,1,0:T(2,128)(2,1)}, u32[]{:S(2)}, u32[]{:S(2)}) collective-permute-start(bf16[5,8,1,512]{3,2,1,0:T(2,128)(2,1)S(1)} %get-tuple-element.56), channel_id=1, source_target_pairs={{0,1},{1,2},{2,3},{3,4},{4,5},{5,6},{6,7},{7,8},{8,9},{9,10},{10,1... | collective-permute-start | bytes 122888 | tf_op jit(solution)/shard_map/ppermute | solution.py:19
  118.5 13.8 %collective-permute-start.1 = (bf16[5,8,1,512]{3,2,1,0:T(2,128)(2,1)S(1)}, bf16[5,8,1,512]{3,2,1,0:T(2,128)(2,1)}, u32[]{:S(2)}, u32[]{:S(2)}) collective-permute-start(bf16[5,8,1,512]{3,2,1,0:T(2,128)(2,1)S(1)} %get-tuple-element.57), channel_id=1, source_target_pairs={{1,0},{2,1},{3,2},{4,3},{5,4},{6,5},{7,6},{8,7},{9,8},{10,9},{11,1... | collective-permute-start | bytes 122888 | tf_op jit(solution)/shard_map/ppermute | solution.py:22
  128.2 4.1 copy-start.4
  136.4 17.2 %all-to-all-start.1 = ((bf16[32,2,2,4]{3,1,2,0:T(2,128)(2,1)}), bf16[32,2,2,4]{3,1,2,0:T(2,128)(2,1)S(1)}, u32[]{:S(2)}, u32[]{:S(2)}) async-start(bf16[32,2,2,4]{3,1,2,0:T(2,128)(2,1)} %copy.43), calls=%async_computation.1 | async-start | bytes 65536 | tf_op jit(solution)/shard_map/all_to_all | solution.py:128
  167.7 250.4 %copy-start.1 = (bf16[12,2048]{1,0:T(8,128)(2,1)S(1)}, bf16[12,2048]{1,0:T(8,128)(2,1)}, u32[]{:S(2)}) copy-start(bf16[12,2048]{1,0:T(8,128)(2,1)} %param.19) | copy-start | bytes 147460
Sparse Core Ops, SparseCore 0:
  10.8 78.7 all-gather.1
  106.0 120.6 all-reduce.1
  229.6 186.8 reduce-scatter.1
where the time goes:
time: 426 us
  waiting for transfers between devices  285 us (67%)
  local copies, waits for them, and re-layouts  41.6 us (10%)
  other arithmetic  33.1 us (8%)
  matrix products  29.2 us (7%)
  starting transfers between devices  20.3 us (5%)
  between operations  16.5 us (4%)
    reduce_scatter x1, waiting for transfers between devices, body(): lax.psum_scatter(contract_first(part, back_second), ('sec', 'dev'), scatt...  190 us
    all_gather x1, waiting for transfers between devices, body(): lax.all_gather(middle_weight, ('sec', 'dev'), axis=0, tiled=True)  44.9 us
    psum x1, waiting for transfers between devices, body(): grad_w_in = lax.psum(contract_first(features, back_first), ('sec', 'dev'))  43.7 us
    dot_general x2, matrix products, contract_first(): lax.dot_general(left, right, (((0,), (0,)), ((), ())), preferred_element_...  17.4 us
    unnamed x27, local copies, waits for them, and re-layouts  14.4 us
    mul x1, other arithmetic, apply_wall(): return advanced.at[3, 0].add(-wall_gain * new_stress[1])  12.3 us
    add x1, other arithmetic, advance(): flow_state + advect_number * (below_x - flow_state)  9.22 us
  transfers between devices with their start and end apart: 8, of which 4 were waited for; matrix products, arithmetic and copies ran while one was open for 20% of the time, Pallas kernels for 0%

commit v1 on v0

--- a/solution.py
+++ b/solution.py
@@ -144,7 +144,9 @@
     grad_w_mid = lax.psum_scatter(
         contract_first(part, back_second), ("sec", "dev"), scatter_dimension=0, tiled=True
     )
-    grad_w_in = lax.psum(contract_first(features, back_first), ("sec", "dev"))
+    own = contract_first(features, back_first)
+    parts = lax.all_gather(own, ("sec", "dev"))
+    grad_w_in = jnp.sum(parts, axis=0)
     per_tile = jnp.einsum("bs,sck->cbk", placing, answers, preferred_element_type=jnp.float32)
     target_index = jnp.where(is_live, wall_index, points).reshape(-1)
     new_stress = (

time: 426 us -> 362 us (0.85)
  waiting for transfers between devices: 285 us -> 218 us
    psum x1 -> x0, waiting for transfers between devices: 43.7 us -> none  [body(): grad_w_in = lax.psum(contract_first(features, back_first), ('sec', 'dev'))]
    reduce_scatter x1, waiting for transfers between devices: 190 us -> 167 us  [body(): lax.psum_scatter(contract_first(part, back_second), ('sec', 'dev'), scatt...]
    unnamed x27 -> x26, local copies, waits for them, and re-layouts: 14.4 us -> 12.9 us
  transfers between devices with their start and end apart: 8 -> 8, of which waited for: 4 -> 3; matrix products, arithmetic and copies ran while one was open for 20% -> 25% of each run, Pallas kernels for 0% -> 0%
where the time goes in v1:
time: 362 us; the launch traced here: 361 us
  waiting for transfers between devices  218 us (60%)
  local copies, waits for them, and re-layouts  40.1 us (11%)
  other arithmetic  36.6 us (10%)
  matrix products  29.2 us (8%)
  starting transfers between devices  20.3 us (6%)
  between operations  16.5 us (5%)
    reduce_scatter x1, waiting for transfers between devices, body(): lax.psum_scatter(contract_first(part, back_second), ('sec', 'dev'), scatt...  167 us
    all_gather x1, waiting for transfers between devices, body(): lax.all_gather(middle_weight, ('sec', 'dev'), axis=0, tiled=True)  45 us
    dot_general x2, matrix products, contract_first(): lax.dot_general(left, right, (((0,), (0,)), ((), ())), preferred_element_...  17.4 us
    unnamed x26, local copies, waits for them, and re-layouts  12.9 us
    mul x1, other arithmetic, apply_wall(): return advanced.at[3, 0].add(-wall_gain * new_stress[1])  12.3 us
    add x1, other arithmetic, advance(): flow_state + advect_number * (below_x - flow_state)  9.62 us
    scatter x1, local copies, waits for them, and re-layouts, body(): new_stress = wall_stress.reshape(2, points).at[:, target_index].set(per_t...  7.6 us
  transfers between devices with their start and end apart: 8, of which 3 were waited for; matrix products, arithmetic and copies ran while one was open for 25% of the time, Pallas kernels for 0%

profile of v1, /device:TPU:9, one launch (start us, length us, event | category | flops | bytes accessed | tf_op | source)
XLA Modules:
  0.0 361.0 jit_solution(15559679086343298229)
XLA Ops:
  7.2 0.7 all-gather.5.cloned.1.call-update
  7.9 0.8 fusion.23
  8.8 0.8 select_reduce_fusion
  9.6 0.7 fusion.34
  10.3 0.8 convolution_convert_fusion.1
  11.2 0.7 copy.49
  11.9 6.3 %all-to-all-start.2 = ((bf16[32,2,4]{2,1,0:T(2,128)(2,1)}), bf16[32,2,4]{2,1,0:T(2,128)(2,1)S(1)}, u32[]{:S(2)}, u32[]{:S(2)}) async-start(bf16[32,2,4]{2,1,0:T(2,128)(2,1)} %bitcast.18), calls=%async_computation.2 | async-start | bytes 32768 | tf_op jit(solution)/shard_map/all_to_all | solution.py:106
  18.2 0.8 copy.37
  19.1 2.0 convert_element_type.52
  21.3 1.0 copy-done.3
  22.3 0.3 copy.53
  22.6 0.2 pad_maximum_fusion.1
  22.9 3.4 copy.38
  26.2 3.4 gather_fusion
  29.7 0.1 copy.39
  29.8 0.2 convolution_convert_fusion
  30.0 0.1 copy.40
  30.1 0.7 copy.41
  30.8 5.8 %all-to-all-start = ((bf16[32,2,14,4]{2,1,3,0:T(2,128)(2,1)}), bf16[32,2,14,4]{2,1,3,0:T(2,128)(2,1)S(1)}, u32[]{:S(2)}, u32[]{:S(2)}) async-start(bf16[32,2,14,4]{2,1,3,0:T(2,128)(2,1)} %copy.41), calls=%async_computation | async-start | bytes 131072 | tf_op jit(solution)/shard_map/all_to_all | solution.py:105
  36.8 5.8 %all-to-all-done = bf16[32,2,14,4]{2,1,3,0:T(2,128)(2,1)S(1)} async-done(((bf16[32,2,14,4]{2,1,3,0:T(2,128)(2,1)}), bf16[32,2,14,4]{2,1,3,0:T(2,128)(2,1)S(1)}, u32[]{:S(2)}, u32[]{:S(2)}) %all-to-all-start) | async-done | bytes 7200 | tf_op jit(solution)/shard_map/all_to_all | solution.py:105
  42.9 1.7 convolution_tanh_fusion.1
  44.6 45.0 %all-gather.5.cloned.1.call-done = bf16[2048,2048]{1,0:T(8,128)(2,1)} async-done(((bf16[64,2048]{1,0:T(8,128)(2,1)}), bf16[2048,2048]{1,0:T(8,128)(2,1)}) %all-gather.5.cloned.1.call-update) | async-done | bytes 8388624 | tf_op jit(solution)/shard_map/all_gather | solution.py:118
  89.6 6.4 %convolution_tanh_fusion = f32[256,2048]{1,0:T(8,128)S(1)} fusion(bf16[2048,2048]{1,0:T(8,128)(2,1)} %all-gather.5.cloned.1.call-done, f32[256,2048]{1,0:T(8,128)} %convolution_tanh_fusion.1), kind=kOutput, calls=%fused_computation.8 | convolution fusion | flops 2148007936 | bytes 12582912 | tf_op jit(solution)/shard_map/dot_general | solution.py:116
  95.9 1.0 multiply_reduce_fusion
  96.9 1.5 fusion.8
  98.4 7.4 %convolution_bitcast_fusion = f32[1,12,2048]{2,1,0:T(8,128)} fusion(bf16[256,2048]{1,0:T(8,128)(2,1)} %fusion.8, bf16[2048,2048]{1,0:T(8,128)(2,1)} %all-gather.5.cloned.1.call-done, f32[256,2048]{1,0:T(8,128)} %convolution_tanh_fusion.1, bf16[256,14]{1,0:T(8,128)(2,1)S(1)} %bitcast.61), kind=kOutput, calls=%fused_computation.21 | convolution fusion | flops 2162163712 | bytes 11639808 | tf_op jit(solution)/shard_map/dot_general | solution.py:51
  105.9 10.0 %fusion.11 = f32[2048,2048]{1,0:T(8,128)} fusion(bf16[256,2048]{1,0:T(8,128)(2,1)} %fusion.8, f32[256,2048]{1,0:T(8,128)} %convolution_tanh_fusion.1), kind=kOutput, calls=%fused_computation.29 | convolution fusion | flops 2148007936 | bytes 19922944 | tf_op jit(solution)/shard_map/dot_general | solution.py:51
  115.9 1.3 fusion.43
  117.1 1.3 collective-permute-start
  118.7 4.6 %copy.35 = f32[2,32,512]{0,2,1:T(8,128)} copy(f32[2,32,512]{2,1,0:T(8,128)S(1)} %copy-done.5) | data formatting | bytes 262144 | tf_op args[2]
  123.3 0.9 fusion.42
  124.3 1.1 fusion.39
  125.4 2.8 fusion.41
  128.1 3.5 fusion.40
  131.6 0.6 convert_reduce_fusion
  132.3 3.3 maximum_convert_fusion
  135.7 0.6 copy.43
  136.3 6.7 %all-to-all-start.1 = ((bf16[32,2,2,4]{3,1,2,0:T(2,128)(2,1)}), bf16[32,2,2,4]{3,1,2,0:T(2,128)(2,1)S(1)}, u32[]{:S(2)}, u32[]{:S(2)}) async-start(bf16[32,2,2,4]{3,1,2,0:T(2,128)(2,1)} %copy.43), calls=%async_computation.1 | async-start | bytes 65536 | tf_op jit(solution)/shard_map/all_to_all | solution.py:128
  143.0 9.6 %fusion.4 = f32[5,8,32,512]{3,2,1,0:T(8,128)} fusion(f32[5,8,34,512]{3,2,1,0:T(8,128)} %maximum_convert_fusion, f32[5,8,32,1]{3,2,1,0:T(8,128)} %get-tuple-element.49, f32[5,8,32,511]{3,2,1,0:T(8,128)} %get-tuple-element.51, f32[5,7,32,512]{3,2,1,0:T(8,128)} %get-tuple-element.53, f32[5,1,32,512]{3,2,1,0:T(8,128)} %get-tuple-element.55, ...), kind=kLoop, calls=%fused_computation.13 | loop fusion | flops 10485760 | bytes 21495808 | tf_op jit(solution)/shard_map/add | solution.py:33
  154.0 0.2 convolution_bitcast_fusion.1
  154.4 0.1 copy.47
  154.5 7.6 %scatter_fusion = f32[2,16384]{0,1:T(8,128)} fusion(f32[2,16384]{0,1:T(8,128)} %bitcast.54, s32[192]{0:T(256)S(1)} %bitcast.70, f32[192,2]{1,0:T(8,128)S(1)} %copy.47), kind=kCustom, calls=%fused_computation.1 | custom fusion | bytes 5376 | tf_op jit(solution)/shard_map/scatter | solution.py:155
  162.1 5.9 %copy.50 = f32[2,32,512]{2,1,0:T(8,128)} copy(f32[2,32,512]{0,2,1:T(8,128)} %bitcast.55) | data formatting | bytes 262144
  168.1 12.3 %fusion = (f32[16384]{0:T(1024)S(1)}, f32[16384]{0:T(1024)S(1)}) fusion(f32[2,16384]{0,1:T(8,128)} %scatter_fusion), kind=kLoop, calls=%fused_computation.3 | loop fusion | flops 32768 | bytes 262144 | tf_op jit(solution)/shard_map/mul | solution.py:47
  180.4 1.5 fusion.15
  181.9 1.5 fusion.14
  183.4 3.1 reduce_sum.42
  186.5 166.9 %reduce-scatter.2.cloned.1.call-done = f32[64,2048]{1,0:T(8,128)} async-done(((f32[2048,2048]{1,0:T(8,128)}), f32[64,2048]{1,0:T(8,128)}) %reduce-scatter.2.cloned.1.call-update) | async-done | bytes 524304 | tf_op jit(solution)/shard_map/reduce_scatter | solution.py:144
  (52 shorter events, 1.5 us)
Async XLA Ops:
  7.2 35.7 %copy-start = (bf16[12,2048]{1,0:T(8,128)(2,1)S(1)}, bf16[12,2048]{1,0:T(8,128)(2,1)}, u32[]{:S(2)}) copy-start(bf16[12,2048]{1,0:T(8,128)(2,1)} %param.19) | copy-start | bytes 147460
  7.2 13.9 %copy-start.2 = (f32[5,8,32,512]{3,2,1,0:T(8,128)S(1)}, f32[5,8,32,512]{3,2,1,0:T(8,128)}, u32[]{:S(2)}) copy-start(f32[5,8,32,512]{3,2,1,0:T(8,128)} %param.13) | copy-start | bytes 7864324
  7.2 82.4 %all-gather.5.cloned.1.call-start = ((), (), s32[]{:S(2)}) async-start(), calls=%async_computation.4 | async-start | bytes 8650752 | tf_op jit(solution)/shard_map/all_gather | solution.py:118
  11.9 18.9 %all-to-all-start.2 = ((bf16[32,2,4]{2,1,0:T(2,128)(2,1)}), bf16[32,2,4]{2,1,0:T(2,128)(2,1)S(1)}, u32[]{:S(2)}, u32[]{:S(2)}) async-start(bf16[32,2,4]{2,1,0:T(2,128)(2,1)} %bitcast.18), calls=%async_computation.2 | async-start | bytes 32768 | tf_op jit(solution)/shard_map/all_to_all | solution.py:106
  21.1 1.1 copy-start.3
  22.8 6.9 %copy-start.7 = (s32[48,4]{0,1:T(4,128)S(1)}, s32[48,4]{0,1:T(4,128)}, u32[]{:S(2)}) copy-start(s32[48,4]{0,1:T(4,128)} %param.18) | copy-start | bytes 2308
  22.8 6.9 %copy-start.8 = (s32[1,48]{1,0:T(1,128)S(1)}, s32[1,48]{1,0:T(1,128)}, u32[]{:S(2)}) copy-start(s32[1,48]{1,0:T(1,128)} %param.16) | copy-start | bytes 580
  30.8 11.8 %all-to-all-start = ((bf16[32,2,14,4]{2,1,3,0:T(2,128)(2,1)}), bf16[32,2,14,4]{2,1,3,0:T(2,128)(2,1)S(1)}, u32[]{:S(2)}, u32[]{:S(2)}) async-start(bf16[32,2,14,4]{2,1,3,0:T(2,128)(2,1)} %copy.41), calls=%async_computation | async-start | bytes 131072 | tf_op jit(solution)/shard_map/all_to_all | solution.py:105
  36.7 146.7 %all-gather.7.cloned.1.call-start = ((), (), s32[]{:S(2)}) async-start(), calls=%async_computation.6 | async-start | bytes 4325376 | tf_op jit(solution)/shard_map/all_gather | solution.py:148
  44.6 51.3 %copy-start.6 = (bf16[2,2048]{1,0:T(2,128)(2,1)S(1)}, bf16[2,2048]{1,0:T(2,128)(2,1)}, u32[]{:S(2)}) copy-start(bf16[2,2048]{1,0:T(2,128)(2,1)} %param.21) | copy-start | bytes 24580
  105.8 247.5 %reduce-scatter.2.cloned.1.call-start = ((), (), s32[]{:S(2)}) async-start(), calls=%async_computation.5 | async-start | bytes 17301504 | tf_op jit(solution)/shard_map/reduce_scatter | solution.py:144
  115.9 2.8 copy-start.5
  117.1 15.1 %collective-permute-start = (bf16[5,8,1,512]{3,2,1,0:T(2,128)(2,1)S(1)}, bf16[5,8,1,512]{3,2,1,0:T(2,128)(2,1)}, u32[]{:S(2)}, u32[]{:S(2)}) collective-permute-start(bf16[5,8,1,512]{3,2,1,0:T(2,128)(2,1)S(1)} %get-tuple-element.56), channel_id=1, source_target_pairs={{0,1},{1,2},{2,3},{3,4},{4,5},{5,6},{6,7},{7,8},{8,9},{9,10},{10,1... | collective-permute-start | bytes 122888 | tf_op jit(solution)/shard_map/ppermute | solution.py:19
  118.5 13.8 %collective-permute-start.1 = (bf16[5,8,1,512]{3,2,1,0:T(2,128)(2,1)S(1)}, bf16[5,8,1,512]{3,2,1,0:T(2,128)(2,1)}, u32[]{:S(2)}, u32[]{:S(2)}) collective-permute-start(bf16[5,8,1,512]{3,2,1,0:T(2,128)(2,1)S(1)} %get-tuple-element.57), channel_id=1, source_target_pairs={{1,0},{2,1},{3,2},{4,3},{5,4},{6,5},{7,6},{8,7},{9,8},{10,9},{11,1... | collective-permute-start | bytes 122888 | tf_op jit(solution)/shard_map/ppermute | solution.py:22
  128.1 4.1 %copy-start.4 = (bf16[5,8,32,512]{3,2,1,0:T(8,128)(2,1)S(1)}, bf16[5,8,32,512]{3,2,1,0:T(8,128)(2,1)}, u32[]{:S(2)}) copy-start(bf16[5,8,32,512]{3,2,1,0:T(8,128)(2,1)} %copy-done.3) | copy-start | bytes 3932164
  136.3 17.6 %all-to-all-start.1 = ((bf16[32,2,2,4]{3,1,2,0:T(2,128)(2,1)}), bf16[32,2,2,4]{3,1,2,0:T(2,128)(2,1)S(1)}, u32[]{:S(2)}, u32[]{:S(2)}) async-start(bf16[32,2,2,4]{3,1,2,0:T(2,128)(2,1)} %copy.43), calls=%async_computation.1 | async-start | bytes 65536 | tf_op jit(solution)/shard_map/all_to_all | solution.py:128
  168.1 185.3 %copy-start.1 = (bf16[12,2048]{1,0:T(8,128)(2,1)S(1)}, bf16[12,2048]{1,0:T(8,128)(2,1)}, u32[]{:S(2)}) copy-start(bf16[12,2048]{1,0:T(8,128)(2,1)} %param.19) | copy-start | bytes 147460
Sparse Core Ops, SparseCore 0:
  10.8 78.6 all-gather.4
  106.0 60.1 all-gather.6
  169.0 184.2 reduce-scatter.1
